TPU v7x, 32 devices: a whole 2x2x4 slice. The times are simulated.
32 devices in a mesh: groups: 2 (over y), ctx: 4 (over z), fsdp: 2 (over x), sub: 2 (over core).
Axes of the slice: x: 2, y: 2, z: 4, core: 2. Of those that a mesh axis runs over, the one named last changes fastest.
Arguments:
- streams: bfloat16 [3, 2048, 4096], P(None, ('groups', 'ctx', 'sub'), 'fsdp'), parts along dimension 1, may hold values from -6 to 6
- feat_taps: float32 [3, 7, 4096], P(None, None, 'fsdp'), may hold values from -2.4 to 2.4
- long_filter: bfloat16 [128, 4096], P('ctx', 'fsdp'), may hold values from -0.5 to 0.5
- upstream: bfloat16 [2048, 4096], P(('groups', 'ctx', 'sub'), 'fsdp'), parts along dimension 0, may hold values from -6 to 6
- score_dir: float32 [4096], P('fsdp'), may hold values from -21 to 21
- seg_lengths: int32 [16], P('groups'), parts along dimension 0, may hold values from 1 to 512, 1024 in all
- list_ids: int32 [16], P('groups'), parts along dimension 0, may hold values from 0 to 1
Outputs:
- d_streams: bfloat16 [3, 2048, 4096], P(None, ('groups', 'ctx', 'sub'), 'fsdp'), parts along dimension 1
- d_feat: float32 [6, 7, 4096], P('groups', None, 'fsdp'), parts along dimension 0
- d_filter: float32 [256, 4096], P(('groups', 'ctx'), 'fsdp'), parts along dimension 0
There are 2 independent parts, one for each index of `groups`. A program takes and returns all parts, laid end to end along the dimension named above; an argument that names none is the same for every part. Nothing has to cross between parts.
Inputs may be any that keep to these rules, and one draw needn't show every extreme that they name: `seg_lengths`: the lengths sum to 1024 and the longest segment has exactly 512 tokens.
All inputs are finite; a program needn't handle non-finite values.
Results may differ from a plain program's by a relative error of at most 0.012.
Values may be sent and summed in bfloat16 or wider, within the bound.
A program may use at most 64 MiB of HBM per device.

v0:
```python
import jax
import jax.numpy as jnp
from jax import lax
from jax.sharding import PartitionSpec as P

LH = 128
KF = 7
HIGH = lax.Precision.HIGHEST


def passed_along(value, axis, steps):
    count = lax.axis_size(axis)
    leading, last = (max(0, -steps), min(count, count - steps))
    return lax.ppermute(value, axis, [(source, source + steps) for source in range(leading, last)])


def tap_block(tap_count):
    return 16 if tap_count % 16 == 0 else tap_count


def segment_age(seg_lengths, positions):
    offsets = jnp.cumsum(seg_lengths, dtype=jnp.int32) - seg_lengths
    member = offsets[None, :] <= positions[:, None]
    seg_index = jnp.sum(member.astype(jnp.int32), axis=1, dtype=jnp.int32) - 1
    seg_start = jnp.max(jnp.where(member, offsets[None, :], 0), axis=1)
    return (seg_index, positions - seg_start)


def causal_taps(tap_table, extended, row_age, tok_rows):
    tap_count = tap_table.shape[0]
    per_turn = tap_block(tap_count)

    def causal_advance(b, running):
        for m in range(per_turn):
            j = b * per_turn + m
            window = lax.dynamic_slice_in_dim(extended, tap_count - 1 - j, tok_rows, 0)
            weight_row = lax.dynamic_index_in_dim(tap_table, j, 0, keepdims=False)
            running = running + jnp.where(
                (row_age >= j)[:, None], weight_row[None, :] * window.astype(jnp.float32), 0.0
            )
        return running

    start_sum = jnp.zeros((tok_rows, extended.shape[1]), jnp.float32)
    return lax.fori_loop(0, tap_count // per_turn, causal_advance, start_sum)


def reverse_taps(tap_table, extended, ext_age, tok_rows):
    tap_count = tap_table.shape[0]
    per_turn = tap_block(tap_count)

    def reverse_advance(b, running):
        for m in range(per_turn):
            j = b * per_turn + m
            window = lax.dynamic_slice_in_dim(extended, j, tok_rows, 0)
            keep = lax.dynamic_slice_in_dim(ext_age, j, tok_rows, 0) >= j
            weight_row = lax.dynamic_index_in_dim(tap_table, j, 0, keepdims=False)
            running = running + jnp.where(
                keep[:, None], weight_row[None, :] * window.astype(jnp.float32), 0.0
            )
        return running

    start_sum = jnp.zeros((tok_rows, extended.shape[1]), jnp.float32)
    return lax.fori_loop(0, tap_count // per_turn, reverse_advance, start_sum)


def correlate_taps(gradient, extended, row_age, tap_count, tok_rows):
    per_turn = tap_block(tap_count)

    def correlate_advance(b, result):
        collected = []
        for m in range(per_turn):
            j = b * per_turn + m
            window = lax.dynamic_slice_in_dim(extended, tap_count - 1 - j, tok_rows, 0)
            product = gradient.astype(jnp.float32) * window.astype(jnp.float32)
            collected.append(jnp.sum(jnp.where((row_age >= j)[:, None], product, 0.0), axis=0))
        return lax.dynamic_update_slice_in_dim(result, jnp.stack(collected), b * per_turn, 0)

    start_rows = jnp.zeros((tap_count, gradient.shape[1]), jnp.float32)
    return lax.fori_loop(0, tap_count // per_turn, correlate_advance, start_rows)


def list_coef(totals, seg_lengths, list_ids):
    length_f = seg_lengths.astype(jnp.float32)
    scores = totals / length_f
    mates = (list_ids[:, None] == list_ids[None, :]).astype(jnp.float32)
    mean_score = jnp.dot(mates, scores, precision=HIGH) / jnp.sum(mates, axis=1)
    return (scores - mean_score) / length_f


def local(streams, feat_taps, long_filter, upstream, score_dir, seg_lengths, list_ids):
    tok_rows = streams.shape[1]
    seg_count = seg_lengths.shape[0]
    first_row = lax.axis_index(("ctx", "sub")) * tok_rows
    positions = first_row + jnp.arange(tok_rows + LH - 1, dtype=jnp.int32)
    seg_span, age_span = segment_age(seg_lengths, positions)
    seg_index = seg_span[:tok_rows]
    row_age = age_span[:tok_rows]
    left_rim = passed_along(streams[:, tok_rows - (KF - 1) :, :], ("ctx", "sub"), 1)
    stream_ext = jnp.concatenate([left_rim, streams], axis=1)
    featured = [
        causal_taps(feat_taps[i], stream_ext[i], row_age, tok_rows).astype(jnp.bfloat16)
        for i in range(3)
    ]
    query, key_feat, value_feat = featured
    product = (key_feat.astype(jnp.float32) * value_feat.astype(jnp.float32)).astype(jnp.bfloat16)
    filt = lax.all_gather(long_filter, "ctx", axis=0, tiled=True).astype(jnp.float32)
    prod_rim = passed_along(product[tok_rows - (LH - 1) :], ("ctx", "sub"), 1)
    prod_ext = jnp.concatenate([prod_rim, product], axis=0)
    mixed = causal_taps(filt, prod_ext, row_age, tok_rows)
    out_y = query.astype(jnp.float32) * mixed
    projected = jnp.dot(out_y, score_dir, precision=HIGH)
    onehot = (seg_index[:, None] == jnp.arange(seg_count, dtype=jnp.int32)[None, :]).astype(
        jnp.float32
    )
    partial_sums = jnp.dot(projected, onehot, precision=HIGH)
    totals = lax.psum(partial_sums, ("ctx", "fsdp", "sub"))
    coef = list_coef(totals, seg_lengths, list_ids)
    tok_coef = jnp.dot(onehot, coef, precision=HIGH)
    d_out = upstream.astype(jnp.float32) + tok_coef[:, None] * score_dir[None, :]
    d_query = (d_out * mixed).astype(jnp.bfloat16)
    d_mixed = (d_out * query.astype(jnp.float32)).astype(jnp.bfloat16)
    grad_rim = passed_along(d_mixed[: LH - 1], ("ctx", "sub"), -1)
    dm_ext = jnp.concatenate([d_mixed, grad_rim], axis=0)
    d_prod = reverse_taps(filt, dm_ext, age_span, tok_rows)
    d_key = (d_prod * value_feat.astype(jnp.float32)).astype(jnp.bfloat16)
    d_value = (d_prod * key_feat.astype(jnp.float32)).astype(jnp.bfloat16)
    filter_part = correlate_taps(d_mixed, prod_ext, row_age, LH, tok_rows)
    grads = jnp.stack([d_query, d_key, d_value])
    feat_rim = passed_along(grads[:, : KF - 1, :], ("ctx", "sub"), -1)
    grads_ext = jnp.concatenate([grads, feat_rim], axis=1)
    d_streams = jnp.stack(
        [reverse_taps(feat_taps[i], grads_ext[i], age_span, tok_rows) for i in range(3)]
    ).astype(jnp.bfloat16)
    taps_part = jnp.stack(
        [correlate_taps(grads[i], stream_ext[i], row_age, KF, tok_rows) for i in range(3)]
    )
    shard_rows = long_filter.shape[0]
    filter_all, d_feat = lax.psum((filter_part, taps_part), ("ctx", "sub"))
    d_filter = lax.dynamic_slice_in_dim(
        filter_all, lax.axis_index("ctx") * shard_rows, shard_rows, 0
    )
    return (d_streams, d_feat, d_filter)


def solution(mesh):
    placed = (
        P(None, ("groups", "ctx", "sub"), "fsdp"),
        P(None, None, "fsdp"),
        P("ctx", "fsdp"),
        P(("groups", "ctx", "sub"), "fsdp"),
        P("fsdp"),
        P("groups"),
        P("groups"),
    )
    return jax.shard_map(
        local,
        mesh=mesh,
        in_specs=placed,
        out_specs=(
            P(None, ("groups", "ctx", "sub"), "fsdp"),
            P("groups", None, "fsdp"),
            P(("groups", "ctx"), "fsdp"),
        ),
        check_vma=False,
    )
```

profile of v0, /device:TPU:0, one launch (start us, length us, event | category | flops | bytes accessed | tf_op | source)
XLA Modules:
  0.0 389.5 jit_solution(13309928368215574927)
XLA Ops:
  15.9 17.6 %all_gather.3 = bf16[128,2048]{1,0:T(8,128)(2,1)S(1)} all-gather(bf16[32,2048]{1,0:T(8,128)(2,1)} %param.15), channel_id=1, replica_groups=mesh['groups'=2,'ctx'=4,'fsdp'=2,'sub'=2] {'ctx'}, dimensions={0}, use_global_device_ids=true | all-gather | bytes 655360 | tf_op jit(solution)/shard_map/all_gather | solution.py:106
  33.4 9.7 %fusion.68 = (bf16[128,2048]{1,0:T(8,128)(2,1)S(1)}, bf16[128,2048]{1,0:T(8,128)(2,1)}, bf16[128,2048]{1,0:T(8,128)(2,1)}, bf16[128,2048]{1,0:T(8,128)(2,1)}) fusion(f32[2048]{0:T(1024)S(1)} %bitcast.486, pred[128]{0:T(512)(128)(4,1)S(1)} %get-tuple-element.922, f32[2048]{0:T(1024)S(1)} %bitcast.488, pred[128]{0:T(512)(128)(4,1)S(1)} %get-tuple-element.921, ...), kind=kLoop, calls=%fused_computation.240 | loop fusion | flops 28311552 | bytes 4907904 | tf_op jit(solution)/shard_map/convert_element_type | solution.py:105
  50.8 68.4 %while.35 = (s32[]{:T(128)}, f32[128,2048]{1,0:T(8,128)}, s32[128]{0:T(128)S(1)}, f32[128,2048]{1,0:T(8,128)}, bf16[255,2048]{1,0:T(8,128)(2,1)S(1)}, /*index=5*...) while((s32[]{:T(128)}, f32[128,2048]{1,0:T(8,128)}, ...), condition=%wide.region_4.5_spmd.clone, body=%wide.region_3.4_spmd.clone.sunk | while | flops 17041540 | bytes 10885599 | solution.py:44
  52.8 5.7 %fusion.242 = f32[128,2048]{1,0:T(8,128)} fusion(f32[128,2048]{1,0:T(8,128)} %get-tuple-element.1254, bf16[255,2048]{1,0:T(8,128)(2,1)S(1)} %get-tuple-element.1297, s32[]{:T(128)S(6)} %select_n.2579, f32[2048]{0:T(1024)S(1)} %bitcast.441, s32[]{:T(128)S(6)} %select_n.2596, f32[2048]{0:T(1024)S(1)} %bitcast.442, s32[]{:T(128)S(6)} %select_n.2597, ...), kind=kLoop, calls=%fused_computation.80.clone.1 | loop fusion | flops 17039360 | bytes 10618945 | tf_op jit(solution)/shard_map/while/body/eval_jaxpr/add | solution.py:38
  60.5 6.7 %fusion.242 = f32[128,2048]{1,0:T(8,128)} fusion(f32[128,2048]{1,0:T(8,128)} %get-tuple-element.1254, bf16[255,2048]{1,0:T(8,128)(2,1)S(1)} %get-tuple-element.1297, s32[]{:T(128)S(6)} %select_n.2579, f32[2048]{0:T(1024)S(1)} %bitcast.441, s32[]{:T(128)S(6)} %select_n.2596, f32[2048]{0:T(1024)S(1)} %bitcast.442, s32[]{:T(128)S(6)} %select_n.2597, ...), kind=kLoop, calls=%fused_computation.80.clone.1 | loop fusion | flops 17039360 | bytes 10618945 | tf_op jit(solution)/shard_map/while/body/eval_jaxpr/add | solution.py:38
  69.0 6.7 %fusion.242 = f32[128,2048]{1,0:T(8,128)} fusion(f32[128,2048]{1,0:T(8,128)} %get-tuple-element.1254, bf16[255,2048]{1,0:T(8,128)(2,1)S(1)} %get-tuple-element.1297, s32[]{:T(128)S(6)} %select_n.2579, f32[2048]{0:T(1024)S(1)} %bitcast.441, s32[]{:T(128)S(6)} %select_n.2596, f32[2048]{0:T(1024)S(1)} %bitcast.442, s32[]{:T(128)S(6)} %select_n.2597, ...), kind=kLoop, calls=%fused_computation.80.clone.1 | loop fusion | flops 17039360 | bytes 10618945 | tf_op jit(solution)/shard_map/while/body/eval_jaxpr/add | solution.py:38
  77.8 6.7 %fusion.242 = f32[128,2048]{1,0:T(8,128)} fusion(f32[128,2048]{1,0:T(8,128)} %get-tuple-element.1254, bf16[255,2048]{1,0:T(8,128)(2,1)S(1)} %get-tuple-element.1297, s32[]{:T(128)S(6)} %select_n.2579, f32[2048]{0:T(1024)S(1)} %bitcast.441, s32[]{:T(128)S(6)} %select_n.2596, f32[2048]{0:T(1024)S(1)} %bitcast.442, s32[]{:T(128)S(6)} %select_n.2597, ...), kind=kLoop, calls=%fused_computation.80.clone.1 | loop fusion | flops 17039360 | bytes 10618945 | tf_op jit(solution)/shard_map/while/body/eval_jaxpr/add | solution.py:38
  86.4 6.7 %fusion.242 = f32[128,2048]{1,0:T(8,128)} fusion(f32[128,2048]{1,0:T(8,128)} %get-tuple-element.1254, bf16[255,2048]{1,0:T(8,128)(2,1)S(1)} %get-tuple-element.1297, s32[]{:T(128)S(6)} %select_n.2579, f32[2048]{0:T(1024)S(1)} %bitcast.441, s32[]{:T(128)S(6)} %select_n.2596, f32[2048]{0:T(1024)S(1)} %bitcast.442, s32[]{:T(128)S(6)} %select_n.2597, ...), kind=kLoop, calls=%fused_computation.80.clone.1 | loop fusion | flops 17039360 | bytes 10618945 | tf_op jit(solution)/shard_map/while/body/eval_jaxpr/add | solution.py:38
  95.1 6.7 %fusion.242 = f32[128,2048]{1,0:T(8,128)} fusion(f32[128,2048]{1,0:T(8,128)} %get-tuple-element.1254, bf16[255,2048]{1,0:T(8,128)(2,1)S(1)} %get-tuple-element.1297, s32[]{:T(128)S(6)} %select_n.2579, f32[2048]{0:T(1024)S(1)} %bitcast.441, s32[]{:T(128)S(6)} %select_n.2596, f32[2048]{0:T(1024)S(1)} %bitcast.442, s32[]{:T(128)S(6)} %select_n.2597, ...), kind=kLoop, calls=%fused_computation.80.clone.1 | loop fusion | flops 17039360 | bytes 10618945 | tf_op jit(solution)/shard_map/while/body/eval_jaxpr/add | solution.py:38
  103.7 6.7 %fusion.242 = f32[128,2048]{1,0:T(8,128)} fusion(f32[128,2048]{1,0:T(8,128)} %get-tuple-element.1254, bf16[255,2048]{1,0:T(8,128)(2,1)S(1)} %get-tuple-element.1297, s32[]{:T(128)S(6)} %select_n.2579, f32[2048]{0:T(1024)S(1)} %bitcast.441, s32[]{:T(128)S(6)} %select_n.2596, f32[2048]{0:T(1024)S(1)} %bitcast.442, s32[]{:T(128)S(6)} %select_n.2597, ...), kind=kLoop, calls=%fused_computation.80.clone.1 | loop fusion | flops 17039360 | bytes 10618945 | tf_op jit(solution)/shard_map/while/body/eval_jaxpr/add | solution.py:38
  112.5 6.7 %fusion.242 = f32[128,2048]{1,0:T(8,128)} fusion(f32[128,2048]{1,0:T(8,128)} %get-tuple-element.1254, bf16[255,2048]{1,0:T(8,128)(2,1)S(1)} %get-tuple-element.1297, s32[]{:T(128)S(6)} %select_n.2579, f32[2048]{0:T(1024)S(1)} %bitcast.441, s32[]{:T(128)S(6)} %select_n.2596, f32[2048]{0:T(1024)S(1)} %bitcast.442, s32[]{:T(128)S(6)} %select_n.2597, ...), kind=kLoop, calls=%fused_computation.80.clone.1 | loop fusion | flops 17039360 | bytes 10618945 | tf_op jit(solution)/shard_map/while/body/eval_jaxpr/add | solution.py:38
  121.5 33.1 %psum.21 = f32[8]{0:T(128)S(1)} all-reduce(f32[8]{0:T(128)S(1)} %convolution_bitcast_fusion.2), channel_id=1, replica_groups=mesh['groups'=2,'ctx'=4,'fsdp'=2,'sub'=2] {'ctx','fsdp','sub'}, use_global_device_ids=true, to_apply=%region_5.6 | all-reduce | flops 8 | bytes 64 | tf_op jit(solution)/shard_map/psum | solution.py:116
  159.8 70.9 %while.34 = (s32[]{:T(128)}, f32[128,2048]{1,0:T(8,128)}, s32[128]{0:T(128)S(1)}, bf16[128,2048]{1,0:T(8,128)(2,1)}, bf16[255,2048]{1,0:T(8,128)(2,1)S(1)}, /*in...) while((s32[]{:T(128)}, f32[128,2048]{1,0:T(8,128)}, ...), condition=%wide.region_48.49_spmd, body=%wide.region_31.48_spmd.sunk | while | flops 17270864 | bytes 10098467 | solution.py:79
  163.7 4.0 %fusion.240 = (f32[2048]{0:T(1024)S(1)}, f32[2048]{0:T(1024)S(1)}, f32[2048]{0:T(1024)S(1)}, f32[2048]{0:T(1024)S(1)}, f32[2048]{0:T(1024)S(1)}, /*index=5*/f32[...) fusion(bf16[128,2048]{1,0:T(8,128)(2,1)} %get-tuple-element.1548, bf16[255,2048]{1,0:T(8,128)(2,1)S(1)} %get-tuple-element.1549, ...), kind=kLoop, calls=%fused_computation.45.clone.1 | loop fusion | flops 8634368 | bytes 4785184 | tf_op jit(solution)/shard_map/while/body/eval_jaxpr/reduce_sum | solution.py:75
  235.4 69.9 %while.36 = (s32[]{:T(128)}, f32[128,2048]{1,0:T(8,128)}, s32[255]{0:T(256)S(1)}, f32[128,2048]{1,0:T(8,128)}, bf16[255,2048]{1,0:T(8,128)(2,1)S(1)}, /*index=5*...) while((s32[]{:T(128)}, f32[128,2048]{1,0:T(8,128)}, ...), condition=%wide.region_8.9_spmd.clone, body=%wide.region_7.8_spmd.clone.sunk | while | flops 17041508 | bytes 10893119 | solution.py:63
  237.5 5.8 %fusion.243 = f32[128,2048]{1,0:T(8,128)} fusion(f32[128,2048]{1,0:T(8,128)} %get-tuple-element.1388, bf16[255,2048]{1,0:T(8,128)(2,1)S(1)} %get-tuple-element.1445, s32[]{:T(128)S(6)} %select_n.2627, f32[2048]{0:T(1024)S(1)} %bitcast.457, s32[]{:T(128)S(6)} %select_n.2644, f32[2048]{0:T(1024)S(1)} %bitcast.458, s32[]{:T(128)S(6)} %select_n.2645, ...), kind=kLoop, calls=%fused_computation.128.clone.1 | loop fusion | flops 17039360 | bytes 10618945 | tf_op jit(solution)/shard_map/while/body/eval_jaxpr/add | solution.py:57
  245.4 6.8 %fusion.243 = f32[128,2048]{1,0:T(8,128)} fusion(f32[128,2048]{1,0:T(8,128)} %get-tuple-element.1388, bf16[255,2048]{1,0:T(8,128)(2,1)S(1)} %get-tuple-element.1445, s32[]{:T(128)S(6)} %select_n.2627, f32[2048]{0:T(1024)S(1)} %bitcast.457, s32[]{:T(128)S(6)} %select_n.2644, f32[2048]{0:T(1024)S(1)} %bitcast.458, s32[]{:T(128)S(6)} %select_n.2645, ...), kind=kLoop, calls=%fused_computation.128.clone.1 | loop fusion | flops 17039360 | bytes 10618945 | tf_op jit(solution)/shard_map/while/body/eval_jaxpr/add | solution.py:57
  254.1 6.8 %fusion.243 = f32[128,2048]{1,0:T(8,128)} fusion(f32[128,2048]{1,0:T(8,128)} %get-tuple-element.1388, bf16[255,2048]{1,0:T(8,128)(2,1)S(1)} %get-tuple-element.1445, s32[]{:T(128)S(6)} %select_n.2627, f32[2048]{0:T(1024)S(1)} %bitcast.457, s32[]{:T(128)S(6)} %select_n.2644, f32[2048]{0:T(1024)S(1)} %bitcast.458, s32[]{:T(128)S(6)} %select_n.2645, ...), kind=kLoop, calls=%fused_computation.128.clone.1 | loop fusion | flops 17039360 | bytes 10618945 | tf_op jit(solution)/shard_map/while/body/eval_jaxpr/add | solution.py:57
  263.1 6.8 %fusion.243 = f32[128,2048]{1,0:T(8,128)} fusion(f32[128,2048]{1,0:T(8,128)} %get-tuple-element.1388, bf16[255,2048]{1,0:T(8,128)(2,1)S(1)} %get-tuple-element.1445, s32[]{:T(128)S(6)} %select_n.2627, f32[2048]{0:T(1024)S(1)} %bitcast.457, s32[]{:T(128)S(6)} %select_n.2644, f32[2048]{0:T(1024)S(1)} %bitcast.458, s32[]{:T(128)S(6)} %select_n.2645, ...), kind=kLoop, calls=%fused_computation.128.clone.1 | loop fusion | flops 17039360 | bytes 10618945 | tf_op jit(solution)/shard_map/while/body/eval_jaxpr/add | solution.py:57
  271.8 6.8 %fusion.243 = f32[128,2048]{1,0:T(8,128)} fusion(f32[128,2048]{1,0:T(8,128)} %get-tuple-element.1388, bf16[255,2048]{1,0:T(8,128)(2,1)S(1)} %get-tuple-element.1445, s32[]{:T(128)S(6)} %select_n.2627, f32[2048]{0:T(1024)S(1)} %bitcast.457, s32[]{:T(128)S(6)} %select_n.2644, f32[2048]{0:T(1024)S(1)} %bitcast.458, s32[]{:T(128)S(6)} %select_n.2645, ...), kind=kLoop, calls=%fused_computation.128.clone.1 | loop fusion | flops 17039360 | bytes 10618945 | tf_op jit(solution)/shard_map/while/body/eval_jaxpr/add | solution.py:57
  280.8 6.8 %fusion.243 = f32[128,2048]{1,0:T(8,128)} fusion(f32[128,2048]{1,0:T(8,128)} %get-tuple-element.1388, bf16[255,2048]{1,0:T(8,128)(2,1)S(1)} %get-tuple-element.1445, s32[]{:T(128)S(6)} %select_n.2627, f32[2048]{0:T(1024)S(1)} %bitcast.457, s32[]{:T(128)S(6)} %select_n.2644, f32[2048]{0:T(1024)S(1)} %bitcast.458, s32[]{:T(128)S(6)} %select_n.2645, ...), kind=kLoop, calls=%fused_computation.128.clone.1 | loop fusion | flops 17039360 | bytes 10618945 | tf_op jit(solution)/shard_map/while/body/eval_jaxpr/add | solution.py:57
  289.5 6.8 %fusion.243 = f32[128,2048]{1,0:T(8,128)} fusion(f32[128,2048]{1,0:T(8,128)} %get-tuple-element.1388, bf16[255,2048]{1,0:T(8,128)(2,1)S(1)} %get-tuple-element.1445, s32[]{:T(128)S(6)} %select_n.2627, f32[2048]{0:T(1024)S(1)} %bitcast.457, s32[]{:T(128)S(6)} %select_n.2644, f32[2048]{0:T(1024)S(1)} %bitcast.458, s32[]{:T(128)S(6)} %select_n.2645, ...), kind=kLoop, calls=%fused_computation.128.clone.1 | loop fusion | flops 17039360 | bytes 10618945 | tf_op jit(solution)/shard_map/while/body/eval_jaxpr/add | solution.py:57
  298.5 6.8 %fusion.243 = f32[128,2048]{1,0:T(8,128)} fusion(f32[128,2048]{1,0:T(8,128)} %get-tuple-element.1388, bf16[255,2048]{1,0:T(8,128)(2,1)S(1)} %get-tuple-element.1445, s32[]{:T(128)S(6)} %select_n.2627, f32[2048]{0:T(1024)S(1)} %bitcast.457, s32[]{:T(128)S(6)} %select_n.2644, f32[2048]{0:T(1024)S(1)} %bitcast.458, s32[]{:T(128)S(6)} %select_n.2645, ...), kind=kLoop, calls=%fused_computation.128.clone.1 | loop fusion | flops 17039360 | bytes 10618945 | tf_op jit(solution)/shard_map/while/body/eval_jaxpr/add | solution.py:57
  326.4 52.9 %all-reduce.3.cloned.1.call-done = (f32[3,7,2048]{2,1,0:T(8,128)}, f32[128,2048]{1,0:T(8,128)}) async-done(((f32[3,7,2048]{2,1,0:T(8,128)}, f32[128,2048]{1,0:T(8,128)}), (f32[3,7,2048]{2,1,0:T(8,128)}, f32[128,2048]{1,0:T(8,128)})) %all-reduce.3.cloned.1.call-update) | async-done | bytes 1220624 | tf_op jit(solution)/shard_map/psum | solution.py:138
  (271 shorter events, 147.7 us)
Async XLA Ops:
  7.2 372.2 %all-reduce.3.cloned.1.call-start = ((), (), s32[]{:S(2)}) async-start(), calls=%async_computation | async-start | bytes 2490368 | tf_op jit(solution)/shard_map/psum | solution.py:138
  8.1 25.3 %collective-permute-start = (bf16[3,6,2048]{2,1,0:T(8,128)(2,1)S(1)}, bf16[3,6,2048]{2,1,0:T(8,128)(2,1)S(1)}, u32[]{:S(2)}, u32[]{:S(2)}) collective-permute-start(bf16[3,6,2048]{2,1,0:T(8,128)(2,1)S(1)} %slice.171), channel_id=1, source_target_pairs={{0,1},{1,4},{4,5},{5,8},{8,9},{9,12},{12,13},{2,3},{3,6},{6,7},{7,... | collective-permute-start | bytes 221192 | tf_op jit(solution)/shard_map/ppermute | solution.py:14
  12.5 35.2 %copy-start.26 = (f32[1,1,2048]{2,1,0:T(1,128)}, f32[1,1,2048]{2,1,0:T(1,128)S(1)}, u32[]{:S(2)}) copy-start(f32[1,1,2048]{2,1,0:T(1,128)S(1)} %get-tuple-element.894) | copy-start | bytes 24580
  12.5 35.2 %copy-start.28 = (f32[1,1,2048]{2,1,0:T(1,128)}, f32[1,1,2048]{2,1,0:T(1,128)S(1)}, u32[]{:S(2)}) copy-start(f32[1,1,2048]{2,1,0:T(1,128)S(1)} %get-tuple-element.907) | copy-start | bytes 24580
  12.5 35.2 %copy-start.30 = (f32[1,1,2048]{2,1,0:T(1,128)}, f32[1,1,2048]{2,1,0:T(1,128)S(1)}, u32[]{:S(2)}) copy-start(f32[1,1,2048]{2,1,0:T(1,128)S(1)} %get-tuple-element.908) | copy-start | bytes 24580
  12.5 35.2 %copy-start.32 = (f32[1,1,2048]{2,1,0:T(1,128)}, f32[1,1,2048]{2,1,0:T(1,128)S(1)}, u32[]{:S(2)}) copy-start(f32[1,1,2048]{2,1,0:T(1,128)S(1)} %get-tuple-element.909) | copy-start | bytes 24580
  12.5 35.2 %copy-start.34 = (f32[1,1,2048]{2,1,0:T(1,128)}, f32[1,1,2048]{2,1,0:T(1,128)S(1)}, u32[]{:S(2)}) copy-start(f32[1,1,2048]{2,1,0:T(1,128)S(1)} %get-tuple-element.910) | copy-start | bytes 24580
  12.5 35.2 %copy-start.36 = (f32[1,1,2048]{2,1,0:T(1,128)}, f32[1,1,2048]{2,1,0:T(1,128)S(1)}, u32[]{:S(2)}) copy-start(f32[1,1,2048]{2,1,0:T(1,128)S(1)} %get-tuple-element.911) | copy-start | bytes 24580
  12.5 35.2 %copy-start.38 = (f32[1,1,2048]{2,1,0:T(1,128)}, f32[1,1,2048]{2,1,0:T(1,128)S(1)}, u32[]{:S(2)}) copy-start(f32[1,1,2048]{2,1,0:T(1,128)S(1)} %get-tuple-element.912) | copy-start | bytes 24580
  15.8 31.9 %copy-start.47 = (pred[128]{0:T(512)(128)(4,1)}, pred[128]{0:T(512)(128)(4,1)S(1)}, u32[]{:S(2)}) copy-start(pred[128]{0:T(512)(128)(4,1)S(1)} %get-tuple-element.922) | copy-start | bytes 388
  15.8 31.9 %copy-start.49 = (pred[128]{0:T(512)(128)(4,1)}, pred[128]{0:T(512)(128)(4,1)S(1)}, u32[]{:S(2)}) copy-start(pred[128]{0:T(512)(128)(4,1)S(1)} %get-tuple-element.917) | copy-start | bytes 388
  15.8 31.9 %copy-start.51 = (pred[128]{0:T(512)(128)(4,1)}, pred[128]{0:T(512)(128)(4,1)S(1)}, u32[]{:S(2)}) copy-start(pred[128]{0:T(512)(128)(4,1)S(1)} %get-tuple-element.918) | copy-start | bytes 388
  15.8 31.9 %copy-start.53 = (pred[128]{0:T(512)(128)(4,1)}, pred[128]{0:T(512)(128)(4,1)S(1)}, u32[]{:S(2)}) copy-start(pred[128]{0:T(512)(128)(4,1)S(1)} %get-tuple-element.919) | copy-start | bytes 388
  15.8 31.9 %copy-start.55 = (pred[128]{0:T(512)(128)(4,1)}, pred[128]{0:T(512)(128)(4,1)S(1)}, u32[]{:S(2)}) copy-start(pred[128]{0:T(512)(128)(4,1)S(1)} %get-tuple-element.920) | copy-start | bytes 388
  15.8 31.9 %copy-start.57 = (pred[128]{0:T(512)(128)(4,1)}, pred[128]{0:T(512)(128)(4,1)S(1)}, u32[]{:S(2)}) copy-start(pred[128]{0:T(512)(128)(4,1)S(1)} %get-tuple-element.921) | copy-start | bytes 388
  44.2 5.4 %collective-permute-start.1 = (bf16[127,2048]{1,0:T(8,128)(2,1)S(1)}, bf16[127,2048]{1,0:T(8,128)(2,1)}, u32[]{:S(2)}, u32[]{:S(2)}) collective-permute-start(bf16[127,2048]{1,0:T(8,128)(2,1)S(1)} %slice.175), channel_id=1, source_target_pairs={{0,1},{1,4},{4,5},{5,8},{8,9},{9,12},{12,13},{2,3},{3,6},{6,7},{7,... | collective-permute-start | bytes 1560584 | tf_op jit(solution)/shard_map/ppermute | solution.py:14
  50.8 68.4 %copy-start.9 = (f32[2048]{0:T(1024)S(1)}, f32[2048]{0:T(1024)}, u32[]{:S(2)}) copy-start(f32[2048]{0:T(1024)} %param.17) | copy-start | bytes 24580
  50.8 103.8 %copy-start.66 = (s32[8]{0:T(128)S(1)}, s32[8]{0:T(128)}, u32[]{:S(2)}) copy-start(s32[8]{0:T(128)} %param.18) | copy-start | bytes 100
  50.8 103.8 %copy-start.68 = (s32[8]{0:T(128)S(1)}, s32[8]{0:T(128)}, u32[]{:S(2)}) copy-start(s32[8]{0:T(128)} %param.19) | copy-start | bytes 100
  157.2 76.8 %collective-permute-start.2 = (bf16[127,2048]{1,0:T(8,128)(2,1)}, bf16[127,2048]{1,0:T(8,128)(2,1)}, u32[]{:S(2)}, u32[]{:S(2)}) collective-permute-start(bf16[127,2048]{1,0:T(8,128)(2,1)} %bitcast.321), channel_id=1, source_target_pairs={{1,0},{4,1},{5,4},{8,5},{9,8},{12,9},{13,12},{3,2},{6,3},{7,6},{10... | collective-permute-start | bytes 1560584 | tf_op jit(solution)/shard_map/ppermute | solution.py:14
  159.8 71.0 %copy-start.4 = (bf16[128,2048]{1,0:T(8,128)(2,1)S(1)}, bf16[128,2048]{1,0:T(8,128)(2,1)}, u32[]{:S(2)}) copy-start(bf16[128,2048]{1,0:T(8,128)(2,1)} %param.16) | copy-start | bytes 1572868
  235.4 69.9 %copy-start.56 = (pred[128]{0:T(512)(128)(4,1)S(1)}, pred[128]{0:T(512)(128)(4,1)}, u32[]{:S(2)}) copy-start(pred[128]{0:T(512)(128)(4,1)} %copy-done.55) | copy-start | bytes 388
  235.4 69.9 %copy-start.58 = (pred[128]{0:T(512)(128)(4,1)S(1)}, pred[128]{0:T(512)(128)(4,1)}, u32[]{:S(2)}) copy-start(pred[128]{0:T(512)(128)(4,1)} %copy-done.57) | copy-start | bytes 388
  310.2 8.9 %collective-permute-start.3 = (bf16[3,6,2048]{2,1,0:T(8,128)(2,1)}, bf16[3,6,2048]{2,1,0:T(8,128)(2,1)S(1)}, u32[]{:S(2)}, u32[]{:S(2)}) collective-permute-start(bf16[3,6,2048]{2,1,0:T(8,128)(2,1)} %pad_maximum_fusion.6), channel_id=1, source_target_pairs={{1,0},{4,1},{5,4},{8,5},{9,8},{12,9},{13,12},{3,2},{6,3},{7,6},{10... | collective-permute-start | bytes 221192 | tf_op jit(solution)/shard_map/ppermute | solution.py:14
  (51 other events, 420.2 us)
Sparse Core Ops, SparseCore 0:
  319.0 60.2 all-reduce.2
where the time goes:
time: 392 us; the launch traced here: 389 us
  other arithmetic  210 us (54%)
  waiting for transfers between devices  52.9 us (13%)
  blocking collectives  50.7 us (13%)
  local copies, waits for them, and re-layouts  46.6 us (12%)
  between operations  15 us (4%)
  starting transfers between devices  7.57 us (2%)
    reduce_sum x21, other arithmetic, correlate_advance(): jnp.sum(jnp.where((row_age >= j)[:, None], product, 0.0), axis=0)  74.8 us
    add x8, other arithmetic, reverse_advance(): running + jnp.where(keep[:, None], weight_row[None, :] * window.astype(jn...  53.1 us
    psum x1, waiting for transfers between devices, local(): filter_all, d_feat = lax.psum((filter_part, taps_part), ('ctx', 'sub'))  52.9 us
    add x8, other arithmetic, causal_advance(): running + jnp.where((row_age >= j)[:, None], weight_row[None, :] * window...  52.7 us
    psum x1, blocking collectives, local(): totals = lax.psum(partial_sums, ('ctx', 'fsdp', 'sub'))  33.1 us
    all_gather x1, blocking collectives, local(): lax.all_gather(long_filter, 'ctx', axis=0, tiled=True).astype(jnp.float32)  17.6 us
    dynamic_slice x9, local copies, waits for them, and re-layouts, reverse_advance(): weight_row = lax.dynamic_index_in_dim(tap_table, j, 0, keepdims=False)  15.9 us
    dynamic_slice x9, local copies, waits for them, and re-layouts, causal_advance(): weight_row = lax.dynamic_index_in_dim(tap_table, j, 0, keepdims=False)  15 us
  transfers between devices with their start and end apart: 5, of which 1 were waited for; matrix products, arithmetic and copies ran while one was open for 25% of the time, Pallas kernels for 0%

commit v1 on v0

--- a/solution.py
+++ b/solution.py
@@ -6,6 +6,10 @@
 LH = 128
 KF = 7
 HIGH = lax.Precision.HIGHEST
+
+
+def register_levels_all(u_in, bus_axis):
+    return lax.all_gather(u_in, bus_axis).sum(axis=0)
 
 
 def passed_along(value, axis, steps):
@@ -113,7 +117,7 @@
         jnp.float32
     )
     partial_sums = jnp.dot(projected, onehot, precision=HIGH)
-    totals = lax.psum(partial_sums, ("ctx", "fsdp", "sub"))
+    totals = register_levels_all(partial_sums, ("ctx", "fsdp", "sub"))
     coef = list_coef(totals, seg_lengths, list_ids)
     tok_coef = jnp.dot(onehot, coef, precision=HIGH)
     d_out = upstream.astype(jnp.float32) + tok_coef[:, None] * score_dir[None, :]

time: 392 us -> 393 us (level)
    psum x1 -> x0, blocking collectives: 33.1 us -> none  [local(): totals = lax.psum(partial_sums, ('ctx', 'fsdp', 'sub'))]
    unnamed x0 -> x1, blocking collectives: none -> 31.4 us
where the time goes in v1:
time: 393 us; the launch traced here: 390 us
  other arithmetic  211 us (54%)
  waiting for transfers between devices  52.9 us (13%)
  blocking collectives  49 us (12%)
  local copies, waits for them, and re-layouts  48 us (12%)
  between operations  15.6 us (4%)
  starting transfers between devices  7.57 us (2%)
    reduce_sum x21, other arithmetic, correlate_advance(): jnp.sum(jnp.where((row_age >= j)[:, None], product, 0.0), axis=0)  74.8 us
    add x8, other arithmetic, reverse_advance(): running + jnp.where(keep[:, None], weight_row[None, :] * window.astype(jn...  53.1 us
    psum x1, waiting for transfers between devices, local(): filter_all, d_feat = lax.psum((filter_part, taps_part), ('ctx', 'sub'))  52.9 us
    add x8, other arithmetic, causal_advance(): running + jnp.where((row_age >= j)[:, None], weight_row[None, :] * window...  52.7 us
    unnamed x1, blocking collectives  31.4 us
    all_gather x1, blocking collectives, local(): lax.all_gather(long_filter, 'ctx', axis=0, tiled=True).astype(jnp.float32)  17.6 us
    dynamic_slice x9, local copies, waits for them, and re-layouts, reverse_advance(): weight_row = lax.dynamic_index_in_dim(tap_table, j, 0, keepdims=False)  15.9 us
    dynamic_slice x9, local copies, waits for them, and re-layouts, causal_advance(): weight_row = lax.dynamic_index_in_dim(tap_table, j, 0, keepdims=False)  15 us
  transfers between devices with their start and end apart: 5, of which 1 were waited for; matrix products, arithmetic and copies ran while one was open for 25% of the time, Pallas kernels for 0%

profile of v1, /device:TPU:0, one launch (start us, length us, event | category | flops | bytes accessed | tf_op | source)
XLA Modules:
  0.0 390.0 jit_solution(6260261182069316988)
XLA Ops:
  15.9 17.6 %all_gather.9 = bf16[128,2048]{1,0:T(8,128)(2,1)S(1)} all-gather(bf16[32,2048]{1,0:T(8,128)(2,1)} %param.15), channel_id=1, replica_groups=mesh['groups'=2,'ctx'=4,'fsdp'=2,'sub'=2] {'ctx'}, dimensions={0}, use_global_device_ids=true | all-gather | bytes 655360 | tf_op jit(solution)/shard_map/all_gather | solution.py:110
  33.4 9.7 %fusion.68 = (bf16[128,2048]{1,0:T(8,128)(2,1)S(1)}, bf16[128,2048]{1,0:T(8,128)(2,1)}, bf16[128,2048]{1,0:T(8,128)(2,1)}, bf16[128,2048]{1,0:T(8,128)(2,1)}) fusion(f32[2048]{0:T(1024)S(1)} %bitcast.487, pred[128]{0:T(512)(128)(4,1)S(1)} %get-tuple-element.922, f32[2048]{0:T(1024)S(1)} %bitcast.489, pred[128]{0:T(512)(128)(4,1)S(1)} %get-tuple-element.921, ...), kind=kLoop, calls=%fused_computation.240 | loop fusion | flops 28311552 | bytes 4907904 | tf_op jit(solution)/shard_map/convert_element_type | solution.py:109
  52.6 68.4 %while.35 = (s32[]{:T(128)}, f32[128,2048]{1,0:T(8,128)}, s32[128]{0:T(128)S(1)}, f32[128,2048]{1,0:T(8,128)}, bf16[255,2048]{1,0:T(8,128)(2,1)S(1)}, /*index=5*...) while((s32[]{:T(128)}, f32[128,2048]{1,0:T(8,128)}, ...), condition=%wide.region_4.5_spmd.clone, body=%wide.region_3.4_spmd.clone.sunk | while | flops 17041540 | bytes 10885599 | solution.py:48
  54.6 5.7 %fusion.242 = f32[128,2048]{1,0:T(8,128)} fusion(f32[128,2048]{1,0:T(8,128)} %get-tuple-element.1254, bf16[255,2048]{1,0:T(8,128)(2,1)S(1)} %get-tuple-element.1297, s32[]{:T(128)S(6)} %select_n.2579, f32[2048]{0:T(1024)S(1)} %bitcast.442, s32[]{:T(128)S(6)} %select_n.2596, f32[2048]{0:T(1024)S(1)} %bitcast.443, s32[]{:T(128)S(6)} %select_n.2597, ...), kind=kLoop, calls=%fused_computation.80.clone.1 | loop fusion | flops 17039360 | bytes 10618945 | tf_op jit(solution)/shard_map/while/body/eval_jaxpr/add | solution.py:42
  62.3 6.7 %fusion.242 = f32[128,2048]{1,0:T(8,128)} fusion(f32[128,2048]{1,0:T(8,128)} %get-tuple-element.1254, bf16[255,2048]{1,0:T(8,128)(2,1)S(1)} %get-tuple-element.1297, s32[]{:T(128)S(6)} %select_n.2579, f32[2048]{0:T(1024)S(1)} %bitcast.442, s32[]{:T(128)S(6)} %select_n.2596, f32[2048]{0:T(1024)S(1)} %bitcast.443, s32[]{:T(128)S(6)} %select_n.2597, ...), kind=kLoop, calls=%fused_computation.80.clone.1 | loop fusion | flops 17039360 | bytes 10618945 | tf_op jit(solution)/shard_map/while/body/eval_jaxpr/add | solution.py:42
  70.8 6.7 %fusion.242 = f32[128,2048]{1,0:T(8,128)} fusion(f32[128,2048]{1,0:T(8,128)} %get-tuple-element.1254, bf16[255,2048]{1,0:T(8,128)(2,1)S(1)} %get-tuple-element.1297, s32[]{:T(128)S(6)} %select_n.2579, f32[2048]{0:T(1024)S(1)} %bitcast.442, s32[]{:T(128)S(6)} %select_n.2596, f32[2048]{0:T(1024)S(1)} %bitcast.443, s32[]{:T(128)S(6)} %select_n.2597, ...), kind=kLoop, calls=%fused_computation.80.clone.1 | loop fusion | flops 17039360 | bytes 10618945 | tf_op jit(solution)/shard_map/while/body/eval_jaxpr/add | solution.py:42
  79.6 6.7 %fusion.242 = f32[128,2048]{1,0:T(8,128)} fusion(f32[128,2048]{1,0:T(8,128)} %get-tuple-element.1254, bf16[255,2048]{1,0:T(8,128)(2,1)S(1)} %get-tuple-element.1297, s32[]{:T(128)S(6)} %select_n.2579, f32[2048]{0:T(1024)S(1)} %bitcast.442, s32[]{:T(128)S(6)} %select_n.2596, f32[2048]{0:T(1024)S(1)} %bitcast.443, s32[]{:T(128)S(6)} %select_n.2597, ...), kind=kLoop, calls=%fused_computation.80.clone.1 | loop fusion | flops 17039360 | bytes 10618945 | tf_op jit(solution)/shard_map/while/body/eval_jaxpr/add | solution.py:42
  88.1 6.7 %fusion.242 = f32[128,2048]{1,0:T(8,128)} fusion(f32[128,2048]{1,0:T(8,128)} %get-tuple-element.1254, bf16[255,2048]{1,0:T(8,128)(2,1)S(1)} %get-tuple-element.1297, s32[]{:T(128)S(6)} %select_n.2579, f32[2048]{0:T(1024)S(1)} %bitcast.442, s32[]{:T(128)S(6)} %select_n.2596, f32[2048]{0:T(1024)S(1)} %bitcast.443, s32[]{:T(128)S(6)} %select_n.2597, ...), kind=kLoop, calls=%fused_computation.80.clone.1 | loop fusion | flops 17039360 | bytes 10618945 | tf_op jit(solution)/shard_map/while/body/eval_jaxpr/add | solution.py:42
  96.9 6.7 %fusion.242 = f32[128,2048]{1,0:T(8,128)} fusion(f32[128,2048]{1,0:T(8,128)} %get-tuple-element.1254, bf16[255,2048]{1,0:T(8,128)(2,1)S(1)} %get-tuple-element.1297, s32[]{:T(128)S(6)} %select_n.2579, f32[2048]{0:T(1024)S(1)} %bitcast.442, s32[]{:T(128)S(6)} %select_n.2596, f32[2048]{0:T(1024)S(1)} %bitcast.443, s32[]{:T(128)S(6)} %select_n.2597, ...), kind=kLoop, calls=%fused_computation.80.clone.1 | loop fusion | flops 17039360 | bytes 10618945 | tf_op jit(solution)/shard_map/while/body/eval_jaxpr/add | solution.py:42
  105.4 6.7 %fusion.242 = f32[128,2048]{1,0:T(8,128)} fusion(f32[128,2048]{1,0:T(8,128)} %get-tuple-element.1254, bf16[255,2048]{1,0:T(8,128)(2,1)S(1)} %get-tuple-element.1297, s32[]{:T(128)S(6)} %select_n.2579, f32[2048]{0:T(1024)S(1)} %bitcast.442, s32[]{:T(128)S(6)} %select_n.2596, f32[2048]{0:T(1024)S(1)} %bitcast.443, s32[]{:T(128)S(6)} %select_n.2597, ...), kind=kLoop, calls=%fused_computation.80.clone.1 | loop fusion | flops 17039360 | bytes 10618945 | tf_op jit(solution)/shard_map/while/body/eval_jaxpr/add | solution.py:42
  114.2 6.7 %fusion.242 = f32[128,2048]{1,0:T(8,128)} fusion(f32[128,2048]{1,0:T(8,128)} %get-tuple-element.1254, bf16[255,2048]{1,0:T(8,128)(2,1)S(1)} %get-tuple-element.1297, s32[]{:T(128)S(6)} %select_n.2579, f32[2048]{0:T(1024)S(1)} %bitcast.442, s32[]{:T(128)S(6)} %select_n.2596, f32[2048]{0:T(1024)S(1)} %bitcast.443, s32[]{:T(128)S(6)} %select_n.2597, ...), kind=kLoop, calls=%fused_computation.80.clone.1 | loop fusion | flops 17039360 | bytes 10618945 | tf_op jit(solution)/shard_map/while/body/eval_jaxpr/add | solution.py:42
  123.6 31.4 %all-reduce = f32[128]{0:T(128)S(1)} all-reduce(f32[128]{0:T(128)S(1)} %dynamic-update-slice), channel_id=2, replica_groups=mesh['groups'=2,'ctx'=4,'fsdp'=2,'sub'=2] {'ctx','fsdp','sub'}, use_global_device_ids=true, to_apply=%add | all-reduce | flops 128 | bytes 1024
  160.3 71.0 %while.34 = (s32[]{:T(128)}, f32[128,2048]{1,0:T(8,128)}, s32[128]{0:T(128)S(1)}, bf16[128,2048]{1,0:T(8,128)(2,1)}, bf16[255,2048]{1,0:T(8,128)(2,1)S(1)}, /*in...) while((s32[]{:T(128)}, f32[128,2048]{1,0:T(8,128)}, ...), condition=%wide.region_48.49_spmd, body=%wide.region_31.48_spmd.sunk | while | flops 17270864 | bytes 10098467 | solution.py:83
  164.2 4.0 %fusion.240 = (f32[2048]{0:T(1024)S(1)}, f32[2048]{0:T(1024)S(1)}, f32[2048]{0:T(1024)S(1)}, f32[2048]{0:T(1024)S(1)}, f32[2048]{0:T(1024)S(1)}, /*index=5*/f32[...) fusion(bf16[128,2048]{1,0:T(8,128)(2,1)} %get-tuple-element.1548, bf16[255,2048]{1,0:T(8,128)(2,1)S(1)} %get-tuple-element.1549, ...), kind=kLoop, calls=%fused_computation.45.clone.1 | loop fusion | flops 8634368 | bytes 4785184 | tf_op jit(solution)/shard_map/while/body/eval_jaxpr/reduce_sum | solution.py:79
  235.9 69.8 %while.36 = (s32[]{:T(128)}, f32[128,2048]{1,0:T(8,128)}, s32[255]{0:T(256)S(1)}, f32[128,2048]{1,0:T(8,128)}, bf16[255,2048]{1,0:T(8,128)(2,1)S(1)}, /*index=5*...) while((s32[]{:T(128)}, f32[128,2048]{1,0:T(8,128)}, ...), condition=%wide.region_8.9_spmd.clone, body=%wide.region_7.8_spmd.clone.sunk | while | flops 17041508 | bytes 10893119 | solution.py:67
  238.0 5.8 %fusion.243 = f32[128,2048]{1,0:T(8,128)} fusion(f32[128,2048]{1,0:T(8,128)} %get-tuple-element.1388, bf16[255,2048]{1,0:T(8,128)(2,1)S(1)} %get-tuple-element.1445, s32[]{:T(128)S(6)} %select_n.2627, f32[2048]{0:T(1024)S(1)} %bitcast.458, s32[]{:T(128)S(6)} %select_n.2644, f32[2048]{0:T(1024)S(1)} %bitcast.459, s32[]{:T(128)S(6)} %select_n.2645, ...), kind=kLoop, calls=%fused_computation.128.clone.1 | loop fusion | flops 17039360 | bytes 10618945 | tf_op jit(solution)/shard_map/while/body/eval_jaxpr/add | solution.py:61
  245.9 6.8 %fusion.243 = f32[128,2048]{1,0:T(8,128)} fusion(f32[128,2048]{1,0:T(8,128)} %get-tuple-element.1388, bf16[255,2048]{1,0:T(8,128)(2,1)S(1)} %get-tuple-element.1445, s32[]{:T(128)S(6)} %select_n.2627, f32[2048]{0:T(1024)S(1)} %bitcast.458, s32[]{:T(128)S(6)} %select_n.2644, f32[2048]{0:T(1024)S(1)} %bitcast.459, s32[]{:T(128)S(6)} %select_n.2645, ...), kind=kLoop, calls=%fused_computation.128.clone.1 | loop fusion | flops 17039360 | bytes 10618945 | tf_op jit(solution)/shard_map/while/body/eval_jaxpr/add | solution.py:61
  254.6 6.8 %fusion.243 = f32[128,2048]{1,0:T(8,128)} fusion(f32[128,2048]{1,0:T(8,128)} %get-tuple-element.1388, bf16[255,2048]{1,0:T(8,128)(2,1)S(1)} %get-tuple-element.1445, s32[]{:T(128)S(6)} %select_n.2627, f32[2048]{0:T(1024)S(1)} %bitcast.458, s32[]{:T(128)S(6)} %select_n.2644, f32[2048]{0:T(1024)S(1)} %bitcast.459, s32[]{:T(128)S(6)} %select_n.2645, ...), kind=kLoop, calls=%fused_computation.128.clone.1 | loop fusion | flops 17039360 | bytes 10618945 | tf_op jit(solution)/shard_map/while/body/eval_jaxpr/add | solution.py:61
  263.6 6.8 %fusion.243 = f32[128,2048]{1,0:T(8,128)} fusion(f32[128,2048]{1,0:T(8,128)} %get-tuple-element.1388, bf16[255,2048]{1,0:T(8,128)(2,1)S(1)} %get-tuple-element.1445, s32[]{:T(128)S(6)} %select_n.2627, f32[2048]{0:T(1024)S(1)} %bitcast.458, s32[]{:T(128)S(6)} %select_n.2644, f32[2048]{0:T(1024)S(1)} %bitcast.459, s32[]{:T(128)S(6)} %select_n.2645, ...), kind=kLoop, calls=%fused_computation.128.clone.1 | loop fusion | flops 17039360 | bytes 10618945 | tf_op jit(solution)/shard_map/while/body/eval_jaxpr/add | solution.py:61
  272.3 6.8 %fusion.243 = f32[128,2048]{1,0:T(8,128)} fusion(f32[128,2048]{1,0:T(8,128)} %get-tuple-element.1388, bf16[255,2048]{1,0:T(8,128)(2,1)S(1)} %get-tuple-element.1445, s32[]{:T(128)S(6)} %select_n.2627, f32[2048]{0:T(1024)S(1)} %bitcast.458, s32[]{:T(128)S(6)} %select_n.2644, f32[2048]{0:T(1024)S(1)} %bitcast.459, s32[]{:T(128)S(6)} %select_n.2645, ...), kind=kLoop, calls=%fused_computation.128.clone.1 | loop fusion | flops 17039360 | bytes 10618945 | tf_op jit(solution)/shard_map/while/body/eval_jaxpr/add | solution.py:61
  281.3 6.8 %fusion.243 = f32[128,2048]{1,0:T(8,128)} fusion(f32[128,2048]{1,0:T(8,128)} %get-tuple-element.1388, bf16[255,2048]{1,0:T(8,128)(2,1)S(1)} %get-tuple-element.1445, s32[]{:T(128)S(6)} %select_n.2627, f32[2048]{0:T(1024)S(1)} %bitcast.458, s32[]{:T(128)S(6)} %select_n.2644, f32[2048]{0:T(1024)S(1)} %bitcast.459, s32[]{:T(128)S(6)} %select_n.2645, ...), kind=kLoop, calls=%fused_computation.128.clone.1 | loop fusion | flops 17039360 | bytes 10618945 | tf_op jit(solution)/shard_map/while/body/eval_jaxpr/add | solution.py:61
  290.0 6.8 %fusion.243 = f32[128,2048]{1,0:T(8,128)} fusion(f32[128,2048]{1,0:T(8,128)} %get-tuple-element.1388, bf16[255,2048]{1,0:T(8,128)(2,1)S(1)} %get-tuple-element.1445, s32[]{:T(128)S(6)} %select_n.2627, f32[2048]{0:T(1024)S(1)} %bitcast.458, s32[]{:T(128)S(6)} %select_n.2644, f32[2048]{0:T(1024)S(1)} %bitcast.459, s32[]{:T(128)S(6)} %select_n.2645, ...), kind=kLoop, calls=%fused_computation.128.clone.1 | loop fusion | flops 17039360 | bytes 10618945 | tf_op jit(solution)/shard_map/while/body/eval_jaxpr/add | solution.py:61
  299.0 6.8 %fusion.243 = f32[128,2048]{1,0:T(8,128)} fusion(f32[128,2048]{1,0:T(8,128)} %get-tuple-element.1388, bf16[255,2048]{1,0:T(8,128)(2,1)S(1)} %get-tuple-element.1445, s32[]{:T(128)S(6)} %select_n.2627, f32[2048]{0:T(1024)S(1)} %bitcast.458, s32[]{:T(128)S(6)} %select_n.2644, f32[2048]{0:T(1024)S(1)} %bitcast.459, s32[]{:T(128)S(6)} %select_n.2645, ...), kind=kLoop, calls=%fused_computation.128.clone.1 | loop fusion | flops 17039360 | bytes 10618945 | tf_op jit(solution)/shard_map/while/body/eval_jaxpr/add | solution.py:61
  326.9 52.9 %all-reduce.4.cloned.1.call-done = (f32[3,7,2048]{2,1,0:T(8,128)}, f32[128,2048]{1,0:T(8,128)}) async-done(((f32[3,7,2048]{2,1,0:T(8,128)}, f32[128,2048]{1,0:T(8,128)}), (f32[3,7,2048]{2,1,0:T(8,128)}, f32[128,2048]{1,0:T(8,128)})) %all-reduce.4.cloned.1.call-update) | async-done | bytes 1220624 | tf_op jit(solution)/shard_map/psum | solution.py:142
  (278 shorter events, 149.2 us)
Async XLA Ops:
  7.2 372.7 %all-reduce.4.cloned.1.call-start = ((), (), s32[]{:S(2)}) async-start(), calls=%async_computation | async-start | bytes 2490368 | tf_op jit(solution)/shard_map/psum | solution.py:142
  8.1 25.3 %collective-permute-start = (bf16[3,6,2048]{2,1,0:T(8,128)(2,1)S(1)}, bf16[3,6,2048]{2,1,0:T(8,128)(2,1)S(1)}, u32[]{:S(2)}, u32[]{:S(2)}) collective-permute-start(bf16[3,6,2048]{2,1,0:T(8,128)(2,1)S(1)} %slice.171), channel_id=1, source_target_pairs={{0,1},{1,4},{4,5},{5,8},{8,9},{9,12},{12,13},{2,3},{3,6},{6,7},{7,... | collective-permute-start | bytes 221192 | tf_op jit(solution)/shard_map/ppermute | solution.py:18
  12.5 36.8 %copy-start.25 = (f32[1,1,2048]{2,1,0:T(1,128)}, f32[1,1,2048]{2,1,0:T(1,128)S(1)}, u32[]{:S(2)}) copy-start(f32[1,1,2048]{2,1,0:T(1,128)S(1)} %get-tuple-element.894) | copy-start | bytes 24580
  12.5 36.8 %copy-start.27 = (f32[1,1,2048]{2,1,0:T(1,128)}, f32[1,1,2048]{2,1,0:T(1,128)S(1)}, u32[]{:S(2)}) copy-start(f32[1,1,2048]{2,1,0:T(1,128)S(1)} %get-tuple-element.907) | copy-start | bytes 24580
  12.5 36.8 %copy-start.29 = (f32[1,1,2048]{2,1,0:T(1,128)}, f32[1,1,2048]{2,1,0:T(1,128)S(1)}, u32[]{:S(2)}) copy-start(f32[1,1,2048]{2,1,0:T(1,128)S(1)} %get-tuple-element.908) | copy-start | bytes 24580
  12.5 36.8 %copy-start.31 = (f32[1,1,2048]{2,1,0:T(1,128)}, f32[1,1,2048]{2,1,0:T(1,128)S(1)}, u32[]{:S(2)}) copy-start(f32[1,1,2048]{2,1,0:T(1,128)S(1)} %get-tuple-element.909) | copy-start | bytes 24580
  12.5 36.8 %copy-start.33 = (f32[1,1,2048]{2,1,0:T(1,128)}, f32[1,1,2048]{2,1,0:T(1,128)S(1)}, u32[]{:S(2)}) copy-start(f32[1,1,2048]{2,1,0:T(1,128)S(1)} %get-tuple-element.910) | copy-start | bytes 24580
  12.5 36.8 %copy-start.35 = (f32[1,1,2048]{2,1,0:T(1,128)}, f32[1,1,2048]{2,1,0:T(1,128)S(1)}, u32[]{:S(2)}) copy-start(f32[1,1,2048]{2,1,0:T(1,128)S(1)} %get-tuple-element.911) | copy-start | bytes 24580
  12.5 36.8 %copy-start.37 = (f32[1,1,2048]{2,1,0:T(1,128)}, f32[1,1,2048]{2,1,0:T(1,128)S(1)}, u32[]{:S(2)}) copy-start(f32[1,1,2048]{2,1,0:T(1,128)S(1)} %get-tuple-element.912) | copy-start | bytes 24580
  15.8 33.5 %copy-start.48 = (pred[128]{0:T(512)(128)(4,1)}, pred[128]{0:T(512)(128)(4,1)S(1)}, u32[]{:S(2)}) copy-start(pred[128]{0:T(512)(128)(4,1)S(1)} %get-tuple-element.917) | copy-start | bytes 388
  15.8 33.6 %copy-start.50 = (pred[128]{0:T(512)(128)(4,1)}, pred[128]{0:T(512)(128)(4,1)S(1)}, u32[]{:S(2)}) copy-start(pred[128]{0:T(512)(128)(4,1)S(1)} %get-tuple-element.918) | copy-start | bytes 388
  15.8 33.6 %copy-start.52 = (pred[128]{0:T(512)(128)(4,1)}, pred[128]{0:T(512)(128)(4,1)S(1)}, u32[]{:S(2)}) copy-start(pred[128]{0:T(512)(128)(4,1)S(1)} %get-tuple-element.919) | copy-start | bytes 388
  15.8 33.6 %copy-start.54 = (pred[128]{0:T(512)(128)(4,1)}, pred[128]{0:T(512)(128)(4,1)S(1)}, u32[]{:S(2)}) copy-start(pred[128]{0:T(512)(128)(4,1)S(1)} %get-tuple-element.920) | copy-start | bytes 388
  15.8 33.6 %copy-start.56 = (pred[128]{0:T(512)(128)(4,1)}, pred[128]{0:T(512)(128)(4,1)S(1)}, u32[]{:S(2)}) copy-start(pred[128]{0:T(512)(128)(4,1)S(1)} %get-tuple-element.921) | copy-start | bytes 388
  44.2 7.0 %collective-permute-start.1 = (bf16[127,2048]{1,0:T(8,128)(2,1)S(1)}, bf16[127,2048]{1,0:T(8,128)(2,1)}, u32[]{:S(2)}, u32[]{:S(2)}) collective-permute-start(bf16[127,2048]{1,0:T(8,128)(2,1)S(1)} %slice.175), channel_id=1, source_target_pairs={{0,1},{1,4},{4,5},{5,8},{8,9},{9,12},{12,13},{2,3},{3,6},{6,7},{7,... | collective-permute-start | bytes 1560584 | tf_op jit(solution)/shard_map/ppermute | solution.py:18
  52.6 68.4 %copy-start.8 = (f32[2048]{0:T(1024)S(1)}, f32[2048]{0:T(1024)}, u32[]{:S(2)}) copy-start(f32[2048]{0:T(1024)} %param.17) | copy-start | bytes 24580
  52.6 70.5 %copy-start.69 = (s32[128]{0:T(128)S(1)}, s32[128]{0:T(128)}, u32[]{:S(2)}) copy-start(s32[128]{0:T(128)} %slice.170) | copy-start | bytes 1540
  121.0 34.1 %copy-start.65 = (s32[8]{0:T(128)S(1)}, s32[8]{0:T(128)}, u32[]{:S(2)}) copy-start(s32[8]{0:T(128)} %param.18) | copy-start | bytes 100
  121.0 34.2 %copy-start.67 = (s32[8]{0:T(128)S(1)}, s32[8]{0:T(128)}, u32[]{:S(2)}) copy-start(s32[8]{0:T(128)} %param.19) | copy-start | bytes 100
  157.7 76.9 %collective-permute-start.2 = (bf16[127,2048]{1,0:T(8,128)(2,1)}, bf16[127,2048]{1,0:T(8,128)(2,1)}, u32[]{:S(2)}, u32[]{:S(2)}) collective-permute-start(bf16[127,2048]{1,0:T(8,128)(2,1)} %bitcast.322), channel_id=1, source_target_pairs={{1,0},{4,1},{5,4},{8,5},{9,8},{12,9},{13,12},{3,2},{6,3},{7,6},{10... | collective-permute-start | bytes 1560584 | tf_op jit(solution)/shard_map/ppermute | solution.py:18
  160.3 71.0 %copy-start.3 = (bf16[128,2048]{1,0:T(8,128)(2,1)S(1)}, bf16[128,2048]{1,0:T(8,128)(2,1)}, u32[]{:S(2)}) copy-start(bf16[128,2048]{1,0:T(8,128)(2,1)} %param.16) | copy-start | bytes 1572868
  235.9 69.9 %copy-start.55 = (pred[128]{0:T(512)(128)(4,1)S(1)}, pred[128]{0:T(512)(128)(4,1)}, u32[]{:S(2)}) copy-start(pred[128]{0:T(512)(128)(4,1)} %copy-done.54) | copy-start | bytes 388
  235.9 69.9 %copy-start.57 = (pred[128]{0:T(512)(128)(4,1)S(1)}, pred[128]{0:T(512)(128)(4,1)}, u32[]{:S(2)}) copy-start(pred[128]{0:T(512)(128)(4,1)} %copy-done.56) | copy-start | bytes 388
  310.7 8.9 %collective-permute-start.3 = (bf16[3,6,2048]{2,1,0:T(8,128)(2,1)}, bf16[3,6,2048]{2,1,0:T(8,128)(2,1)S(1)}, u32[]{:S(2)}, u32[]{:S(2)}) collective-permute-start(bf16[3,6,2048]{2,1,0:T(8,128)(2,1)} %pad_maximum_fusion.6), channel_id=1, source_target_pairs={{1,0},{4,1},{5,4},{8,5},{9,8},{12,9},{13,12},{3,2},{6,3},{7,6},{10... | collective-permute-start | bytes 221192 | tf_op jit(solution)/shard_map/ppermute | solution.py:18
  (52 other events, 458.5 us)
Sparse Core Ops, SparseCore 0:
  319.5 60.2 all-reduce.3
